TPU v7x, 32 devices: a whole 2x2x4 slice. The times are simulated.
32 devices in a mesh: rows: 8 (over z, x), grp: 4 (over y, core).
Axes of the slice: x: 2, y: 2, z: 4, core: 2. Of those that a mesh axis runs over, the one named last changes fastest.
Arguments:
- bin_codes: int32 [131072, 512], P(('rows', 'grp')), may hold values from 0 to 31
- leaf_index: int32 [131072, 1], P(('rows', 'grp')), may hold values from 0 to 7; in each aligned block of 4096 rows (0 to 4095, 4096 to 8191, ...) at most 1024 rows name the same one
- gradients: bfloat16 [131072, 16], P(('rows', 'grp')), may hold values from -6 to 6
- row_weights: bfloat16 [131072], P(('rows', 'grp')), may hold values from 0.5 to 2
- split_feature: int32 [1], replicated, may hold values from 0 to 511
- split_bin: int32 [1], replicated, may hold values from 0 to 30
Outputs:
- gain_table: float32 [16384], P('rows')
- best_gain: float32 [1], replicated
- moved_gradients: bfloat16 [64, 65536], P(('rows', 'grp'))
- moved_weights: bfloat16 [64, 4096], P(('rows', 'grp'))
Inputs may be any that keep to these rules, and one draw needn't show every extreme that they name: `leaf_index`: among the rows of one device, each leaf holds at most 1024 rows, and some leaf holds exactly 1024 on some devices.
All inputs are finite; a program needn't handle non-finite values.
Results may differ from a plain program's by a relative error of at most 0.0004.
Values may be sent and summed in bfloat16 or wider, within the bound.
A program may use at most 128 MiB of HBM per device.

v0:
```python
import math

import jax
import jax.numpy as jnp
from jax import lax
from jax.sharding import PartitionSpec as P

BINS = 32
TARGETS = 16
LEAVES = 8
CAP = 1024


ridge = 1.0


def split_scores(grad_hist, weight_hist):
    left_g = jnp.cumsum(grad_hist, axis=1)
    left_w = jnp.cumsum(weight_hist, axis=1)
    upper_g = jnp.flip(jnp.cumsum(jnp.flip(grad_hist, axis=1), axis=1), axis=1)
    upper_w = jnp.flip(jnp.cumsum(jnp.flip(weight_hist, axis=1), axis=1), axis=1)
    right_g = jnp.concatenate([upper_g[:, 1:], jnp.zeros_like(upper_g[:, :1])], axis=1)
    right_w = jnp.concatenate([upper_w[:, 1:], jnp.zeros_like(upper_w[:, :1])], axis=1)
    left_x = left_w + ridge
    right_y = right_w + ridge
    diff = left_g * right_y[..., None] - right_g * left_x[..., None]
    terms = diff * diff / (left_x * right_y * (left_x + right_y))[..., None]
    return jnp.sum(terms, axis=(2, 3)) / (LEAVES * TARGETS)


def place_rows(leaf, child, grads, weights):
    key_ids = leaf * 2 + child
    key_hot = (key_ids[:, None] == jnp.arange(2 * LEAVES, dtype=jnp.int32)[None, :]).astype(
        jnp.int32
    )
    before = jnp.cumsum(key_hot, axis=0) - key_hot
    rank = jnp.sum(before * key_hot, axis=1)
    counts = jnp.sum(key_hot, axis=0)
    leaf_hot = (leaf[:, None] == jnp.arange(LEAVES, dtype=jnp.int32)[None, :]).astype(jnp.int32)
    first = jnp.sum(leaf_hot * counts[0::2][None, :], axis=1)
    slot = leaf * CAP + rank + child * first
    buf_g = jnp.zeros((LEAVES * CAP, grads.shape[1]), grads.dtype).at[slot].set(grads)
    buf_w = jnp.zeros((LEAVES * CAP,), weights.dtype).at[slot].set(weights)
    return (buf_g.reshape(LEAVES, CAP * grads.shape[1]), buf_w.reshape(LEAVES, CAP))


def owned_gains(grad_sum, weight_sum):
    grad_hist = grad_sum.reshape(-1, BINS, LEAVES, TARGETS)
    weight_hist = weight_sum.reshape(-1, BINS, LEAVES)
    return split_scores(grad_hist, weight_hist).reshape(-1)


def histograms(codes, leaf, grads, weights, step):
    row_count = codes.shape[0]
    feature_count = codes.shape[1]
    width = math.gcd(64, feature_count)
    block_count = feature_count // width
    turns = row_count // step
    leaf_hot = (leaf[:, None] == jnp.arange(LEAVES, dtype=jnp.int32)[None, :]).astype(jnp.bfloat16)
    grad_cols = (leaf_hot[:, :, None] * grads[:, None, :]).reshape(row_count, LEAVES * TARGETS)
    weight_cols = leaf_hot * weights[:, None]
    bin_ids = jnp.arange(BINS, dtype=jnp.int32)
    dims = (((0,), (0,)), ((), ()))

    def one_block(index):
        codes_block = lax.dynamic_slice_in_dim(codes, index * width, width, 1)

        def add_rows(carry, turn):
            bin_hot = (
                (codes_block[:, :, None] == bin_ids[None, None, :])
                .astype(jnp.bfloat16)
                .reshape(step, width * BINS)
            )
            grad_part = lax.dot_general(
                bin_hot, grad_cols, dims, preferred_element_type=jnp.float32
            )
            weight_part = lax.dot_general(
                bin_hot, weight_cols, dims, preferred_element_type=jnp.float32
            )
            return ((carry[0] + grad_part, carry[1] + weight_part), None)

        start_sums = (
            jnp.zeros((width * BINS, LEAVES * TARGETS), jnp.float32),
            jnp.zeros((width * BINS, LEAVES), jnp.float32),
        )
        sums, unused = lax.scan(add_rows, start_sums, jnp.arange(turns, dtype=jnp.int32))
        return sums

    grad_term, weight_term = lax.map(one_block, jnp.arange(block_count, dtype=jnp.int32))
    return (
        grad_term.reshape(feature_count * BINS, LEAVES * TARGETS),
        weight_term.reshape(feature_count * BINS, LEAVES),
    )


def shards(bin_codes, leaf_index, gradients, row_weights, split_feature, split_bin):
    local_rows = bin_codes.shape[0]
    leaf = leaf_index[:, 0]
    column = lax.dynamic_slice_in_dim(bin_codes, split_feature[0], 1, 1)[:, 0]
    child = (column > split_bin[0]).astype(jnp.int32)
    send_g, send_w = place_rows(leaf, child, gradients, row_weights)
    moved_gradients, moved_weights = (
        lax.all_to_all(send_g, "grp", split_axis=0, concat_axis=1, tiled=True),
        lax.all_to_all(send_w, "grp", split_axis=0, concat_axis=1, tiled=True),
    )
    grad_term, weight_term = histograms(bin_codes, leaf, gradients, row_weights, local_rows)
    grad_sum, weight_sum = (
        lax.psum_scatter(grad_term, ("rows", "grp"), scatter_dimension=0, tiled=True),
        lax.psum_scatter(weight_term, ("rows", "grp"), scatter_dimension=0, tiled=True),
    )
    gain_local = owned_gains(grad_sum, weight_sum)
    gain_table = lax.all_gather(gain_local, "grp", axis=0, tiled=True)
    best_gain = lax.pmax(jnp.max(gain_table), "rows").reshape(1)
    return (gain_table, best_gain, moved_gradients, moved_weights)


def solution(mesh):
    placed = (
        P(("rows", "grp"), None),
        P(("rows", "grp"), None),
        P(("rows", "grp"), None),
        P(("rows", "grp")),
        P(),
        P(),
    )
    return jax.shard_map(
        shards,
        mesh=mesh,
        in_specs=placed,
        out_specs=(P("rows"), P(), P(("rows", "grp"), None), P(("rows", "grp"), None)),
        check_vma=False,
    )
```

profile of v0, /device:TPU:0, one launch (start us, length us, event | category | flops | bytes accessed | tf_op | source)
XLA Modules:
  0.0 537.3 jit_solution(1026792904070890021)
XLA Ops:
  7.3 9.0 %copy.38 = s32[4096,512]{0,1:T(8,128)} copy(s32[4096,512]{1,0:T(8,128)} %param.8) | data formatting | bytes 16777216
  16.3 149.7 %while.13 = (s32[]{:T(128)}, f32[8,2048,128]{2,1,0:T(8,128)}, f32[8,2048,8]{1,2,0:T(8,128)}, s32[8]{0:T(128)S(1)}, s32[4096,512]{0,1:T(8,128)}, /*index=5*/bf16[...) while((s32[]{:T(128)}, f32[8,2048,128]{2,1,0:T(8,128)}, ...), condition=%wide.region_1.2_spmd.clone, body=%wide.region_0.0_spmd.clone.sunk | while | flops 2290679808 | bytes 31776972 | solution.py:89
  19.0 5.3 bitcast_compare_fusion.2
  24.4 5.6 %fusion.45 = f32[8,2048,128]{2,1,0:T(8,128)} fusion(f32[8,2048,128]{2,1,0:T(8,128)} %get-tuple-element.215, s32[]{:T(128)S(6)} %copy.56, pred[4096,2048]{0,1:T(32,128)(4,1)S(1)} %bitcast_compare_fusion.2, bf16[4096,128]{0,1:T(8,128)(2,1)S(1)} %bitcast.72), kind=kOutput, calls=%fused_computation.7.clone.1 | convolution fusion | flops 2147483648 | bytes 10485764 | tf_op jit(solution)/shard_map/while/body/eval_jaxpr/while/body/eval_jaxpr/dot_general | solution.py:74
  30.0 5.1 fusion.46
  36.4 1.3 constant_dynamic-slice_fusion.2
  37.7 5.3 bitcast_compare_fusion.2
  43.1 5.7 %fusion.45 = f32[8,2048,128]{2,1,0:T(8,128)} fusion(f32[8,2048,128]{2,1,0:T(8,128)} %get-tuple-element.215, s32[]{:T(128)S(6)} %copy.56, pred[4096,2048]{0,1:T(32,128)(4,1)S(1)} %bitcast_compare_fusion.2, bf16[4096,128]{0,1:T(8,128)(2,1)S(1)} %bitcast.72), kind=kOutput, calls=%fused_computation.7.clone.1 | convolution fusion | flops 2147483648 | bytes 10485764 | tf_op jit(solution)/shard_map/while/body/eval_jaxpr/while/body/eval_jaxpr/dot_general | solution.py:74
  48.8 5.0 fusion.46
  56.4 5.3 bitcast_compare_fusion.2
  61.8 5.6 %fusion.45 = f32[8,2048,128]{2,1,0:T(8,128)} fusion(f32[8,2048,128]{2,1,0:T(8,128)} %get-tuple-element.215, s32[]{:T(128)S(6)} %copy.56, pred[4096,2048]{0,1:T(32,128)(4,1)S(1)} %bitcast_compare_fusion.2, bf16[4096,128]{0,1:T(8,128)(2,1)S(1)} %bitcast.72), kind=kOutput, calls=%fused_computation.7.clone.1 | convolution fusion | flops 2147483648 | bytes 10485764 | tf_op jit(solution)/shard_map/while/body/eval_jaxpr/while/body/eval_jaxpr/dot_general | solution.py:74
  67.5 5.0 fusion.46
  75.1 5.3 bitcast_compare_fusion.2
  80.5 5.6 %fusion.45 = f32[8,2048,128]{2,1,0:T(8,128)} fusion(f32[8,2048,128]{2,1,0:T(8,128)} %get-tuple-element.215, s32[]{:T(128)S(6)} %copy.56, pred[4096,2048]{0,1:T(32,128)(4,1)S(1)} %bitcast_compare_fusion.2, bf16[4096,128]{0,1:T(8,128)(2,1)S(1)} %bitcast.72), kind=kOutput, calls=%fused_computation.7.clone.1 | convolution fusion | flops 2147483648 | bytes 10485764 | tf_op jit(solution)/shard_map/while/body/eval_jaxpr/while/body/eval_jaxpr/dot_general | solution.py:74
  86.2 5.0 fusion.46
  93.8 5.3 bitcast_compare_fusion.2
  99.2 5.6 %fusion.45 = f32[8,2048,128]{2,1,0:T(8,128)} fusion(f32[8,2048,128]{2,1,0:T(8,128)} %get-tuple-element.215, s32[]{:T(128)S(6)} %copy.56, pred[4096,2048]{0,1:T(32,128)(4,1)S(1)} %bitcast_compare_fusion.2, bf16[4096,128]{0,1:T(8,128)(2,1)S(1)} %bitcast.72), kind=kOutput, calls=%fused_computation.7.clone.1 | convolution fusion | flops 2147483648 | bytes 10485764 | tf_op jit(solution)/shard_map/while/body/eval_jaxpr/while/body/eval_jaxpr/dot_general | solution.py:74
  104.8 5.0 fusion.46
  112.5 5.3 bitcast_compare_fusion.2
  117.9 5.6 %fusion.45 = f32[8,2048,128]{2,1,0:T(8,128)} fusion(f32[8,2048,128]{2,1,0:T(8,128)} %get-tuple-element.215, s32[]{:T(128)S(6)} %copy.56, pred[4096,2048]{0,1:T(32,128)(4,1)S(1)} %bitcast_compare_fusion.2, bf16[4096,128]{0,1:T(8,128)(2,1)S(1)} %bitcast.72), kind=kOutput, calls=%fused_computation.7.clone.1 | convolution fusion | flops 2147483648 | bytes 10485764 | tf_op jit(solution)/shard_map/while/body/eval_jaxpr/while/body/eval_jaxpr/dot_general | solution.py:74
  123.6 5.0 fusion.46
  131.3 5.3 bitcast_compare_fusion.2
  136.7 5.6 %fusion.45 = f32[8,2048,128]{2,1,0:T(8,128)} fusion(f32[8,2048,128]{2,1,0:T(8,128)} %get-tuple-element.215, s32[]{:T(128)S(6)} %copy.56, pred[4096,2048]{0,1:T(32,128)(4,1)S(1)} %bitcast_compare_fusion.2, bf16[4096,128]{0,1:T(8,128)(2,1)S(1)} %bitcast.72), kind=kOutput, calls=%fused_computation.7.clone.1 | convolution fusion | flops 2147483648 | bytes 10485764 | tf_op jit(solution)/shard_map/while/body/eval_jaxpr/while/body/eval_jaxpr/dot_general | solution.py:74
  142.3 5.0 fusion.46
  150.0 5.3 bitcast_compare_fusion.2
  155.4 5.6 %fusion.45 = f32[8,2048,128]{2,1,0:T(8,128)} fusion(f32[8,2048,128]{2,1,0:T(8,128)} %get-tuple-element.215, s32[]{:T(128)S(6)} %copy.56, pred[4096,2048]{0,1:T(32,128)(4,1)S(1)} %bitcast_compare_fusion.2, bf16[4096,128]{0,1:T(8,128)(2,1)S(1)} %bitcast.72), kind=kOutput, calls=%fused_computation.7.clone.1 | convolution fusion | flops 2147483648 | bytes 10485764 | tf_op jit(solution)/shard_map/while/body/eval_jaxpr/while/body/eval_jaxpr/dot_general | solution.py:74
  161.0 5.0 fusion.46
  166.3 9.0 %copy.39 = f32[16384,128]{0,1:T(8,128)} copy(f32[16384,128]{1,0:T(8,128)} %bitcast.73) | data formatting | bytes 16777216 | tf_op jit(solution)/shard_map/reshape | solution.py:91
  177.6 4.6 reduce-window.6
  184.5 28.6 %scatter_custom_fusion.1 = bf16[8192]{0:T(1024)(128)(2,1)S(1)} fusion(s32[4096]{0:T(1024)S(1)} %bitcast.88, bf16[4096]{0:T(1024)(128)(2,1)S(1)} %get-tuple-element.261, bf16[]{:T(256)} %constant.26.clone.1), kind=kCustom, calls=%fused_computation.43 | custom fusion | bytes 16386 | tf_op jit(solution)/shard_map/scatter | solution.py:43
  213.7 4.3 all-to-all-start.1
  217.9 1.3 copy.48
  219.3 11.9 %scatter_custom_fusion = bf16[8192,16]{1,0:T(8,128)(2,1)S(1)} fusion(s32[4096]{0:T(1024)S(1)} %bitcast.89, bf16[4096,16]{1,0:T(8,128)(2,1)} %copy.48, bf16[]{:T(256)} %constant.26.clone.1), kind=kCustom, calls=%fused_computation.21 | custom fusion | bytes 262656 | tf_op jit(solution)/shard_map/scatter | solution.py:42
  231.1 2.9 all_to_all.28
  234.0 3.6 all-to-all-start
  237.6 6.0 %all-to-all-done = bf16[4,2,16384]{2,1,0:T(2,128)(2,1)S(1)} async-done(((bf16[4,2,16384]{2,1,0:T(2,128)(2,1)}), bf16[4,2,16384]{2,1,0:T(2,128)(2,1)S(1)}, u32[]{:S(2)}, u32[]{:S(2)}) %all-to-all-start) | async-done | bytes 262176 | tf_op jit(solution)/shard_map/all_to_all | solution.py:103
  243.6 61.2 %reduce-scatter.5.cloned.1.call-done = f32[512,8]{0,1:T(8,128)} async-done(((f32[16384,8]{0,1:T(8,128)}), f32[512,8]{0,1:T(8,128)}) %reduce-scatter.5.cloned.1.call-update) | async-done | bytes 16400 | tf_op jit(solution)/shard_map/reduce_scatter | solution.py:109
  306.1 1.9 fusion.26
  308.0 2.1 pad_add_fusion
  311.8 141.2 %reduce-scatter.3.cloned.1.call-done = f32[512,128]{0,1:T(8,128)} async-done(((f32[16384,128]{0,1:T(8,128)}), f32[512,128]{0,1:T(8,128)}) %reduce-scatter.3.cloned.1.call-update) | async-done | bytes 262160 | tf_op jit(solution)/shard_map/reduce_scatter | solution.py:108
  456.4 3.2 copy.43
  459.6 1.7 fusion.27
  461.3 1.5 slice.29
  462.8 3.0 slice.24
  465.8 30.0 %fusion.25 = f32[16,32,8,16]{3,2,1,0:T(8,128)S(1)} fusion(f32[16,32,8,16]{3,2,1,0:T(8,128)S(1)} %copy.40), kind=kOutput, calls=%fused_computation.46 | output fusion | flops 2031616 | bytes 524288 | tf_op jit(solution)/shard_map/jit(cumsum)/reduce_window_sum | solution.py:18
  495.8 9.1 %fusion.14 = f32[16,32]{1,0:T(8,128)S(1)} fusion(f32[16,31,8,16]{3,2,1,0:T(8,128)S(1)} %copy-done, f32[16,32,8,16]{3,2,1,0:T(8,128)S(1)} %fusion.25, f32[16,32,8]{2,1,0:T(8,128)S(1)} %copy.46, f32[16,32,8]{2,1,0:T(8,128)S(1)} %copy-done.2, f32[16,32,8]{2,1,0:T(8,128)S(1)} %copy-done.3), kind=kLoop, calls=%fused_computation.19 | loop fusion | flops 392704 | bytes 567296 | tf_op jit(solution)/shard_map/reduce_sum | solution.py:28
  505.0 5.2 all-gather
  510.8 17.7 %pmax.7 = f32[1]{0:T(128)} all-reduce(f32[1]{0:T(128)} %bitcast.4), channel_id=1, replica_groups=mesh['rows'=8,'grp'=4] {'rows'}, use_global_device_ids=true, to_apply=%region_10.11 | all-reduce | flops 1 | bytes 8 | tf_op jit(solution)/shard_map/pmax | solution.py:113
  (92 shorter events, 28.2 us)
Async XLA Ops:
  7.2 297.7 %reduce-scatter.5.cloned.1.call-start = ((), (), s32[]{:S(2)}) async-start(), calls=%async_computation.5 | async-start | bytes 540672 | tf_op jit(solution)/shard_map/reduce_scatter | solution.py:109
  7.2 9.0 %copy-start.6 = (s32[4096,1]{0,1:T(1,128)S(1)}, s32[4096,1]{0,1:T(1,128)}, u32[]{:S(2)}) copy-start(s32[4096,1]{0,1:T(1,128)} %param.9) | copy-start | bytes 49156
  7.2 9.1 %copy-start.1 = (bf16[4096,16]{0,1:T(8,128)(2,1)S(1)}, bf16[4096,16]{0,1:T(8,128)(2,1)}, u32[]{:S(2)}) copy-start(bf16[4096,16]{0,1:T(8,128)(2,1)} %param.10) | copy-start | bytes 393220
  7.3 9.1 %copy-start.7 = (bf16[4096]{0:T(1024)(128)(2,1)S(1)}, bf16[4096]{0:T(1024)(128)(2,1)}, u32[]{:S(2)}) copy-start(bf16[4096]{0:T(1024)(128)(2,1)} %param.11) | copy-start | bytes 24580
  166.1 286.9 %reduce-scatter.3.cloned.1.call-start = ((), (), s32[]{:S(2)}) async-start(), calls=%async_computation.4 | async-start | bytes 8650752 | tf_op jit(solution)/shard_map/reduce_scatter | solution.py:108
  213.7 20.3 %all-to-all-start.1 = ((bf16[4,2,1024]{2,1,0:T(2,128)(2,1)}), bf16[4,2,1024]{2,1,0:T(2,128)(2,1)S(1)}, u32[]{:S(2)}, u32[]{:S(2)}) async-start(bf16[4,2,1024]{2,1,0:T(2,128)(2,1)} %all_to_all.32), calls=%async_computation.3 | async-start | bytes 32768 | tf_op jit(solution)/shard_map/all_to_all | solution.py:104
  234.0 9.6 %all-to-all-start = ((bf16[4,2,16384]{2,1,0:T(2,128)(2,1)}), bf16[4,2,16384]{2,1,0:T(2,128)(2,1)S(1)}, u32[]{:S(2)}, u32[]{:S(2)}) async-start(bf16[4,2,16384]{2,1,0:T(2,128)(2,1)} %all_to_all.28), calls=%async_computation.2 | async-start | bytes 524288 | tf_op jit(solution)/shard_map/all_to_all | solution.py:103
  243.6 62.0 %copy-start.4 = (bf16[4,2,16384]{2,1,0:T(2,128)(2,1)}, bf16[4,2,16384]{2,1,0:T(2,128)(2,1)S(1)}, u32[]{:S(2)}) copy-start(bf16[4,2,16384]{2,1,0:T(2,128)(2,1)S(1)} %all-to-all-done) | copy-start | bytes 786436
  465.7 30.0 %copy-start = (f32[16,31,8,16]{3,2,1,0:T(8,128)S(1)}, f32[16,31,8,16]{3,2,1,0:T(8,128)}, u32[]{:S(2)}) copy-start(f32[16,31,8,16]{3,2,1,0:T(8,128)} %slice.24) | copy-start | bytes 761860
  465.8 30.0 %copy-start.2 = (f32[16,32,8]{2,1,0:T(8,128)S(1)}, f32[16,32,8]{2,1,0:T(8,128)}, u32[]{:S(2)}) copy-start(f32[16,32,8]{2,1,0:T(8,128)} %copy.45) | copy-start | bytes 49156
  465.8 30.0 %copy-start.3 = (f32[16,32,8]{2,1,0:T(8,128)S(1)}, f32[16,32,8]{2,1,0:T(8,128)}, u32[]{:S(2)}) copy-start(f32[16,32,8]{2,1,0:T(8,128)} %copy.42) | copy-start | bytes 49156
  495.8 33.4 %copy-start.5 = (bf16[4,2,16384]{2,1,0:T(2,128)(2,1)S(1)}, bf16[4,2,16384]{2,1,0:T(2,128)(2,1)}, u32[]{:S(2)}) copy-start(bf16[4,2,16384]{2,1,0:T(2,128)(2,1)} %copy-done.4) | copy-start | bytes 786436
Sparse Core Ops, SparseCore 0:
  166.2 138.6 reduce-scatter.4
  307.1 145.8 reduce-scatter.2
where the time goes:
time: 539 us; the launch traced here: 537 us
  waiting for transfers between devices  208 us (39%)
  other arithmetic  95.8 us (18%)
  local copies, waits for them, and re-layouts  95.5 us (18%)
  matrix products  85.4 us (16%)
  blocking collectives  22.9 us (4%)
  between operations  15.6 us (3%)
  starting transfers between devices  8.14 us (2%)
  loops' own time  5.45 us (1%)
    reduce_scatter x1, waiting for transfers between devices, shards(): lax.psum_scatter(grad_term, ('rows', 'grp'), scatter_dimension=0, tiled=T...  141 us
    reduce_scatter x1, waiting for transfers between devices, shards(): lax.psum_scatter(weight_term, ('rows', 'grp'), scatter_dimension=0, tiled...  61.2 us
    dot_general x8, matrix products, add_rows(): lax.dot_general(bin_hot, grad_cols, dims, preferred_element_type=jnp.floa...  45 us
    eq x8, other arithmetic, add_rows(): codes_block[:, :, None] == bin_ids[None, None, :]  42.4 us
    dot_general x8, matrix products, add_rows(): lax.dot_general(bin_hot, weight_cols, dims, preferred_element_type=jnp.fl...  40.4 us
    another operation x1, other arithmetic, split_scores(): left_g = jnp.cumsum(grad_hist, axis=1)  30 us
    scatter x1, local copies, waits for them, and re-layouts, place_rows(): buf_w = jnp.zeros((LEAVES * CAP,), weights.dtype).at[slot].set(weights)  28.6 us
    pmax x1, blocking collectives, shards(): best_gain = lax.pmax(jnp.max(gain_table), 'rows').reshape(1)  17.7 us
  transfers between devices with their start and end apart: 4, of which 3 were waited for; matrix products, arithmetic and copies ran while one was open for 12% of the time, Pallas kernels for 0%

commit v1 on v0

v1 whole, which is shorter than its diff:
```python
import functools

import jax
import jax.numpy as jnp
from jax import lax
from jax.experimental import pallas as pl
from jax.experimental.pallas import tpu as pltpu
from jax.sharding import PartitionSpec as P

BINS = 32
TARGETS = 16
LEAVES = 8
CAP = 1024
LANES = 128
CHUNKS = 4
ridge = 1.0
VMEM_LIMIT = 56 * 1024 * 1024
NT = (((1,), (1,)), ((), ()))


def params(**kw):
    return pltpu.CompilerParams(vmem_limit_bytes=VMEM_LIMIT, **kw)


def prep_kernel(feat_ref, codes_ref, leaf_ref, grad_ref, weight_ref, turned_ref, column_ref, data_ref):
    turned = codes_ref[...].astype(jnp.float32).T.astype(jnp.bfloat16)
    turned_ref[...] = turned
    features = turned.shape[0]
    pick = lax.broadcasted_iota(jnp.int32, (8, features), 1) == feat_ref[0]
    pick = jnp.where(pick, 1.0, 0.0).astype(jnp.bfloat16)
    column_ref[...] = jnp.dot(pick, turned, preferred_element_type=jnp.float32)
    leaf = leaf_ref[...]
    step = leaf.shape[1]
    grads = grad_ref[...].astype(jnp.float32)
    parts = [jnp.where(leaf == l, grads, 0.0) for l in range(LEAVES)]
    ids = lax.broadcasted_iota(jnp.int32, (LANES, step), 0)
    parts.append(jnp.where(ids == leaf, weight_ref[...].astype(jnp.float32), 0.0))
    data_ref[...] = jnp.concatenate(parts, axis=0).T.astype(jnp.bfloat16)


def partition_kernel(bin_ref, leaf_ref, column_ref, grad_ref, weight_ref, out_g_ref, out_w_ref):
    keys = 2 * LEAVES
    rows = leaf_ref.shape[1]
    leaf = leaf_ref[...]
    child = jnp.where(column_ref[0:1, :] > bin_ref[0].astype(jnp.float32), 1, 0)
    key = leaf * 2 + child
    hot = jnp.where(lax.broadcasted_iota(jnp.int32, (keys, rows), 0) == key, 1.0, 0.0)
    counts = jnp.sum(hot, axis=1, keepdims=True)
    key_ids = lax.broadcasted_iota(jnp.int32, (keys, 1), 0)
    base = jnp.where(key_ids % 2 == 1, pltpu.roll(jnp.broadcast_to(counts, (keys, LANES)), 1, 0)[:, 0:1], 0.0)
    base = base + (key_ids // 2 * CAP).astype(jnp.float32)
    width = 256
    upper = jnp.where(
        lax.broadcasted_iota(jnp.int32, (width, width), 0)
        < lax.broadcasted_iota(jnp.int32, (width, width), 1),
        1.0,
        0.0,
    ).astype(jnp.bfloat16)
    slots = []
    for c in range(rows // width):
        part = hot[:, c * width : (c + 1) * width]
        rank = jnp.dot(part.astype(jnp.bfloat16), upper, preferred_element_type=jnp.float32)
        slots.append(jnp.sum(part * (rank + base), axis=0, keepdims=True))
        base = base + jnp.sum(part, axis=1, keepdims=True)
    per = LANES // TARGETS
    group = LEAVES * CAP // per
    pages = LEAVES * CAP // LANES
    wide = 512
    acc_g = jnp.zeros((group, LANES), jnp.float32)
    acc_w = jnp.zeros((pages, LANES), jnp.float32)
    for c in range(rows // wide):
        many = wide // width
        slot = jnp.concatenate(slots[c * many : (c + 1) * many], axis=1).astype(jnp.int32)
        span = slice(c * wide, (c + 1) * wide)
        grads = grad_ref[:, span].astype(jnp.float32)
        lhs = jnp.where(
            lax.broadcasted_iota(jnp.int32, (group, wide), 0) == slot // per, 1.0, 0.0
        ).astype(jnp.bfloat16)
        rest = slot % per
        rhs = jnp.concatenate([jnp.where(rest == k, grads, 0.0) for k in range(per)], axis=0)
        acc_g += lax.dot_general(lhs, rhs.astype(jnp.bfloat16), NT, preferred_element_type=jnp.float32)
        lhs = jnp.where(
            lax.broadcasted_iota(jnp.int32, (pages, wide), 0) == slot // LANES, 1.0, 0.0
        ).astype(jnp.bfloat16)
        rhs = jnp.where(
            lax.broadcasted_iota(jnp.int32, (LANES, wide), 0) == slot % LANES,
            weight_ref[:, span].astype(jnp.float32),
            0.0,
        ).astype(jnp.bfloat16)
        acc_w += lax.dot_general(lhs, rhs, NT, preferred_element_type=jnp.float32)
    out_g_ref[...] = acc_g.astype(jnp.bfloat16)
    out_w_ref[...] = acc_w.astype(jnp.bfloat16)


def hist_kernel(first, count, owners, turned_ref, data_ref, out_ref, w_ref):
    features = turned_ref.shape[0]
    own = features // owners
    w_ref[...] = jnp.zeros_like(w_ref)

    def one_bin(b, carry):
        which = (first + b).astype(jnp.float32).astype(jnp.bfloat16)
        hot = jnp.where(turned_ref[...] == which, 1.0, 0.0).astype(jnp.bfloat16)
        both = jnp.dot(hot, data_ref[...], preferred_element_type=jnp.float32)
        for d in range(owners):
            out_ref[d, b] = both[d * own : (d + 1) * own, :LANES]
        w_ref[...] += pltpu.roll(both[:, LANES:], b * LEAVES, 1)
        return carry

    lax.fori_loop(0, count, one_bin, 0)
    for d in range(owners):
        out_ref[d, count] = w_ref[d * own : (d + 1) * own, :]


def gain_kernel(count, *refs):
    parts, out_ref = refs[:-1], refs[-1]
    own = out_ref.shape[0]
    left_g, left_w = [], []
    row = lax.broadcasted_iota(jnp.int32, (LANES, LANES), 0)
    col = lax.broadcasted_iota(jnp.int32, (LANES, LANES), 1)
    grad_hist, weight_hist = [], []
    for part in parts:
        weights = part[count]
        for b in range(count):
            spread = jnp.where(row == b * LEAVES + col // TARGETS, 1.0, 0.0)
            grad_hist.append(part[b])
            weight_hist.append(
                jnp.dot(weights, spread, precision=lax.Precision.HIGHEST, preferred_element_type=jnp.float32)
            )
    bins = len(grad_hist)
    right_g = [jnp.zeros_like(grad_hist[0])] * bins
    right_w = [jnp.zeros_like(weight_hist[0])] * bins
    for b in range(bins - 2, -1, -1):
        right_g[b] = right_g[b + 1] + grad_hist[b + 1]
        right_w[b] = right_w[b + 1] + weight_hist[b + 1]
    lane = lax.broadcasted_iota(jnp.int32, (own, LANES), 1)
    table = jnp.zeros((own, LANES), jnp.float32)
    left_g = jnp.zeros_like(grad_hist[0])
    left_w = jnp.zeros_like(weight_hist[0])
    for b in range(bins):
        left_g = left_g + grad_hist[b]
        left_w = left_w + weight_hist[b]
        x = left_w + ridge
        y = right_w[b] + ridge
        diff = left_g * y - right_g[b] * x
        terms = diff * diff / (x * y * (x + y))
        score = jnp.sum(terms, axis=1, keepdims=True) / (LEAVES * TARGETS)
        table = jnp.where(lane == b, score, table)
    out_ref[...] = table


def shards(owners, bin_codes, leaf_index, gradients, row_weights, split_feature, split_bin):
    rows, features = bin_codes.shape
    leaf = leaf_index.T
    grads = gradients.T
    weights = row_weights.reshape(1, rows)
    step = 512
    vm = pl.BlockSpec(memory_space=pltpu.VMEM)
    sm = pl.BlockSpec(memory_space=pltpu.SMEM)
    turned, column, data = pl.pallas_call(
        prep_kernel,
        grid=(rows // step,),
        in_specs=[
            sm,
            pl.BlockSpec((step, features), lambda i: (i, 0)),
            pl.BlockSpec((1, step), lambda i: (0, i)),
            pl.BlockSpec((TARGETS, step), lambda i: (0, i)),
            pl.BlockSpec((1, step), lambda i: (0, i)),
        ],
        out_specs=[
            pl.BlockSpec((features, step), lambda i: (0, i)),
            pl.BlockSpec((8, step), lambda i: (0, i)),
            pl.BlockSpec((step, 2 * LANES), lambda i: (i, 0)),
        ],
        out_shape=[
            jax.ShapeDtypeStruct((features, rows), jnp.bfloat16),
            jax.ShapeDtypeStruct((8, rows), jnp.float32),
            jax.ShapeDtypeStruct((rows, 2 * LANES), jnp.bfloat16),
        ],
        compiler_params=params(),
        name="prep",
    )(split_feature, bin_codes, leaf, grads, weights)

    per = LANES // TARGETS
    send_g, send_w = pl.pallas_call(
        partition_kernel,
        in_specs=[sm, vm, vm, vm, vm],
        out_specs=[vm, vm],
        out_shape=[
            jax.ShapeDtypeStruct((LEAVES * CAP // per, LANES), jnp.bfloat16),
            jax.ShapeDtypeStruct((LEAVES * CAP // LANES, LANES), jnp.bfloat16),
        ],
        compiler_params=params(),
        name="partition",
    )(split_bin, leaf, column, grads, weights)
    send_g = send_g.reshape(LEAVES, CAP * TARGETS)
    send_w = send_w.reshape(LEAVES, CAP)
    moved_gradients = lax.all_to_all(send_g, "grp", split_axis=0, concat_axis=1, tiled=True)
    moved_weights = lax.all_to_all(send_w, "grp", split_axis=0, concat_axis=1, tiled=True)

    count = BINS // CHUNKS
    own = features // owners
    parts = []
    for c in range(CHUNKS):
        term = pl.pallas_call(
            functools.partial(hist_kernel, c * count, count, owners),
            in_specs=[vm, vm],
            out_specs=vm,
            out_shape=jax.ShapeDtypeStruct((owners, count + 1, own, LANES), jnp.float32),
            scratch_shapes=[pltpu.VMEM((features, LANES), jnp.float32)],
            compiler_params=params(),
            cost_estimate=pl.CostEstimate(
                flops=4 * features * count * rows * LANES, bytes_accessed=8 << 20, transcendentals=0
            ),
            name="hist",
        )(turned, data)
        parts.append(
            lax.psum_scatter(term, ("rows", "grp"), scatter_dimension=0, tiled=True).reshape(
                count + 1, own, LANES
            )
        )
    table = pl.pallas_call(
        functools.partial(gain_kernel, count),
        in_specs=[vm] * CHUNKS,
        out_specs=vm,
        out_shape=jax.ShapeDtypeStruct((own, LANES), jnp.float32),
        compiler_params=params(),
        name="gain",
    )(*parts)
    gain_local = table[:, :BINS].reshape(-1)
    everything = lax.all_gather(gain_local, ("rows", "grp"), axis=0, tiled=True)
    best_gain = jnp.max(everything).reshape(1)
    share = everything.shape[0] // lax.axis_size("rows")
    gain_table = lax.dynamic_slice_in_dim(everything, lax.axis_index("rows") * share, share, 0)
    return (gain_table, best_gain, moved_gradients, moved_weights)


def solution(mesh):
    placed = (
        P(("rows", "grp"), None),
        P(("rows", "grp"), None),
        P(("rows", "grp"), None),
        P(("rows", "grp")),
        P(),
        P(),
    )
    return jax.shard_map(
        functools.partial(shards, mesh.shape["rows"] * mesh.shape["grp"]),
        mesh=mesh,
        in_specs=placed,
        out_specs=(P("rows"), P(), P(("rows", "grp"), None), P(("rows", "grp"), None)),
        check_vma=False,
    )
```

time: 539 us -> 501 us (0.929)
  waiting for transfers between devices: 208 us -> 353 us
  other arithmetic: 95.8 us -> 0.73 us
  local copies, waits for them, and re-layouts: 95.5 us -> 7.04 us
  matrix products: 85.4 us -> 0 us
  Pallas kernels: 0 us -> 77.3 us
  blocking collectives: 22.9 us -> 39.6 us
  loops' own time: 5.45 us -> 0 us
    reduce_scatter x2 -> x4, waiting for transfers between devices: 202 us -> 345 us  [shards(): lax.psum_scatter(term, ('rows', 'grp'), scatter_dimension=0, tiled=True)]
    dot_general x16 -> x0, matrix products: 85.4 us -> none  [the longest x8 45 us: add_rows(): lax.dot_general(bin_hot, grad_cols, dims, preferred_element_type=jnp.floa...]
    pallas_call x0 -> x7, Pallas kernels: none -> 77.3 us  [the longest x4 59.9 us: shards(): pl.pallas_call(functools.partial(hist_kernel, c * count, count, owners),...]
    eq x8 -> x0, other arithmetic: 42.4 us -> none  [add_rows(): codes_block[:, :, None] == bin_ids[None, None, :]]
    another operation x7 -> x0, other arithmetic: 40.6 us -> none  [the longest x1 30 us: split_scores(): left_g = jnp.cumsum(grad_hist, axis=1)]
    scatter x2 -> x0, local copies, waits for them, and re-layouts: 40.4 us -> none  [the longest x1 28.6 us: place_rows(): buf_w = jnp.zeros((LEAVES * CAP,), weights.dtype).at[slot].set(weights)]
    all_gather x1, blocking collectives: 5.19 us -> 39.6 us  [shards(): everything = lax.all_gather(gain_local, ('rows', 'grp'), axis=0, tiled=True)]
    pmax x1 -> x0, blocking collectives: 17.7 us -> none  [shards(): best_gain = lax.pmax(jnp.max(gain_table), 'rows').reshape(1)]
  transfers between devices with their start and end apart: 4 -> 6, of which waited for: 3 -> 6; matrix products, arithmetic and copies ran while one was open for 12% -> 0% of each run, Pallas kernels for 0% -> 10%
where the time goes in v1:
time: 501 us
  waiting for transfers between devices  353 us (70%)
  Pallas kernels  77.3 us (15%)
  blocking collectives  39.6 us (8%)
  between operations  15.1 us (3%)
  starting transfers between devices  7.84 us (2%)
  local copies, waits for them, and re-layouts  7.04 us (1%)
    reduce_scatter x4, waiting for transfers between devices, shards(): lax.psum_scatter(term, ('rows', 'grp'), scatter_dimension=0, tiled=True)  345 us
    pallas_call x4, Pallas kernels, shards(): pl.pallas_call(functools.partial(hist_kernel, c * count, count, owners),...  59.9 us
    all_gather x1, blocking collectives, shards(): everything = lax.all_gather(gain_local, ('rows', 'grp'), axis=0, tiled=True)  39.6 us
  transfers between devices with their start and end apart: 6, of which 6 were waited for; matrix products, arithmetic and copies ran while one was open for 0% of the time, Pallas kernels for 10%

profile of v1, /device:TPU:0, one launch (start us, length us, event | category | flops | bytes accessed | tf_op | source)
XLA Modules:
  0.0 500.6 jit_solution(4813127368768116894)
XLA Ops:
  7.2 0.0 reduce-scatter.11.cloned.1.call-start
  7.2 1.3 reshape.39.weight_ref
  9.2 9.0 %prep.1 = (bf16[512,4096]{1,0:T(8,128)(2,1)}, f32[8,4096]{1,0:T(8,128)}, bf16[4096,256]{1,0:T(8,128)(2,1)}) custom-call(s32[1]{0:T(128)S(6)} %copy.16.feat_ref, s32[4096,512]{1,0:T(8,128)} %codes_ref.1, s32[1,4096]{1,0:T(1,128)} %bitcast.23, bf16[16,4096]{1,0:T(8,128)(2,1)} %bitcast.16, bf16[1,4096]{1,0:T(2,128)(2,1)} %reshape.39.weight_ref), custom_call_target="tpu_custom_call" | custom-call | tf_op jit(solution)/shard_map/prep/pallas_call | solution.py:159
  18.2 14.9 %hist.7 = f32[32,9,16,128]{3,2,1,0:T(8,128)} custom-call(bf16[512,4096]{1,0:T(8,128)(2,1)} %get-tuple-element.9.turned_ref, bf16[4096,256]{1,0:T(8,128)(2,1)} %get-tuple-element.10.data_ref), custom_call_target="tpu_custom_call" | custom-call | flops 8589934592 | bytes 8388608 | tf_op jit(solution)/shard_map/hist/pallas_call | solution.py:204
  33.1 0.0 reduce-scatter.11.cloned.1.call-update
  33.2 0.0 reduce-scatter.9.cloned.1.call-start
  33.2 14.9 %hist.6 = f32[32,9,16,128]{3,2,1,0:T(8,128)} custom-call(bf16[512,4096]{1,0:T(8,128)(2,1)} %get-tuple-element.9.turned_ref, bf16[4096,256]{1,0:T(8,128)(2,1)} %get-tuple-element.10.data_ref), custom_call_target="tpu_custom_call" | custom-call | flops 8589934592 | bytes 8388608 | tf_op jit(solution)/shard_map/hist/pallas_call | solution.py:204
  48.1 0.0 reduce-scatter.9.cloned.1.call-update
  48.2 0.0 reduce-scatter.7.cloned.1.call-start
  48.2 15.0 %hist.5 = f32[32,9,16,128]{3,2,1,0:T(8,128)} custom-call(bf16[512,4096]{1,0:T(8,128)(2,1)} %get-tuple-element.9.turned_ref, bf16[4096,256]{1,0:T(8,128)(2,1)} %get-tuple-element.10.data_ref), custom_call_target="tpu_custom_call" | custom-call | flops 8589934592 | bytes 8388608 | tf_op jit(solution)/shard_map/hist/pallas_call | solution.py:204
  63.2 0.0 reduce-scatter.7.cloned.1.call-update
  63.2 0.0 reduce-scatter.5.cloned.1.call-start
  63.3 15.0 %hist.4 = f32[32,9,16,128]{3,2,1,0:T(8,128)} custom-call(bf16[512,4096]{1,0:T(8,128)(2,1)} %get-tuple-element.9.turned_ref, bf16[4096,256]{1,0:T(8,128)(2,1)} %get-tuple-element.10.data_ref), custom_call_target="tpu_custom_call" | custom-call | flops 8589934592 | bytes 8388608 | tf_op jit(solution)/shard_map/hist/pallas_call | solution.py:204
  78.3 0.0 reduce-scatter.5.cloned.1.call-update
  79.0 4.8 partition.1
  83.8 1.3 all_to_all.32
  85.1 4.3 all-to-all-start.1
  89.4 1.7 all_to_all.28
  91.1 2.2 all-to-all-done.1
  93.2 3.4 all-to-all-start
  96.7 6.0 %all-to-all-done = bf16[4,2,16384]{2,1,0:T(2,128)(2,1)S(1)} async-done(((bf16[4,2,16384]{2,1,0:T(2,128)(2,1)}), bf16[4,2,16384]{2,1,0:T(2,128)(2,1)S(1)}, u32[]{:S(2)}, u32[]{:S(2)}) %all-to-all-start) | async-done | bytes 262176 | tf_op jit(solution)/shard_map/all_to_all | solution.py:197
  102.6 33.1 %reduce-scatter.11.cloned.1.call-done = f32[1,9,16,128]{3,2,1,0:T(8,128)} async-done(((f32[32,9,16,128]{3,2,1,0:T(8,128)}), f32[1,9,16,128]{3,2,1,0:T(8,128)}) %reduce-scatter.11.cloned.1.call-update) | async-done | bytes 73744 | tf_op jit(solution)/shard_map/reduce_scatter | solution.py:217
  135.7 103.9 %reduce-scatter.9.cloned.1.call-done = f32[1,9,16,128]{3,2,1,0:T(8,128)} async-done(((f32[32,9,16,128]{3,2,1,0:T(8,128)}), f32[1,9,16,128]{3,2,1,0:T(8,128)}) %reduce-scatter.9.cloned.1.call-update) | async-done | bytes 73744 | tf_op jit(solution)/shard_map/reduce_scatter | solution.py:217
  239.6 103.9 %reduce-scatter.7.cloned.1.call-done = f32[1,9,16,128]{3,2,1,0:T(8,128)} async-done(((f32[32,9,16,128]{3,2,1,0:T(8,128)}), f32[1,9,16,128]{3,2,1,0:T(8,128)}) %reduce-scatter.7.cloned.1.call-update) | async-done | bytes 73744 | tf_op jit(solution)/shard_map/reduce_scatter | solution.py:217
  343.5 103.9 %reduce-scatter.5.cloned.1.call-done = f32[1,9,16,128]{3,2,1,0:T(8,128)} async-done(((f32[32,9,16,128]{3,2,1,0:T(8,128)}), f32[1,9,16,128]{3,2,1,0:T(8,128)}) %reduce-scatter.5.cloned.1.call-update) | async-done | bytes 73744 | tf_op jit(solution)/shard_map/reduce_scatter | solution.py:217
  447.4 3.6 gain.1
  451.0 0.8 reshape.46
  451.7 39.6 %all-gather = f32[32,1,512]{2,1,0:T(1,128)S(1)} all-gather(f32[1,1,512]{2,1,0:T(1,128)S(1)} %reshape.46), channel_id=1, replica_groups=mesh['rows'=8,'grp'=4] {'rows','grp'}, dimensions={0}, use_global_device_ids=true | all-gather | bytes 67584 | tf_op jit(solution)/shard_map/all_gather | solution.py:230
  491.4 0.7 reduce_max.9
  492.1 0.6 dynamic_slice.3
  492.7 0.7 copy.18
  493.4 0.6 copy.19
Async XLA Ops:
  7.2 128.5 %reduce-scatter.11.cloned.1.call-start = ((), (), s32[]{:S(2)}) async-start(), calls=%async_computation.9 | async-start | bytes 2433024 | tf_op jit(solution)/shard_map/reduce_scatter | solution.py:217
  33.2 206.5 %reduce-scatter.9.cloned.1.call-start = ((), (), s32[]{:S(2)}) async-start(), calls=%async_computation.8 | async-start | bytes 2433024 | tf_op jit(solution)/shard_map/reduce_scatter | solution.py:217
  48.2 295.4 %reduce-scatter.7.cloned.1.call-start = ((), (), s32[]{:S(2)}) async-start(), calls=%async_computation.7 | async-start | bytes 2433024 | tf_op jit(solution)/shard_map/reduce_scatter | solution.py:217
  63.2 384.2 %reduce-scatter.5.cloned.1.call-start = ((), (), s32[]{:S(2)}) async-start(), calls=%async_computation.6 | async-start | bytes 2433024 | tf_op jit(solution)/shard_map/reduce_scatter | solution.py:217
  85.1 8.1 %all-to-all-start.1 = ((bf16[4,2,1024]{2,1,0:T(2,128)(2,1)}), bf16[4,2,1024]{2,1,0:T(2,128)(2,1)S(1)}, u32[]{:S(2)}, u32[]{:S(2)}) async-start(bf16[4,2,1024]{2,1,0:T(2,128)(2,1)} %all_to_all.32), calls=%async_computation.5 | async-start | bytes 32768 | tf_op jit(solution)/shard_map/all_to_all | solution.py:198
  93.2 9.4 %all-to-all-start = ((bf16[4,2,16384]{2,1,0:T(2,128)(2,1)}), bf16[4,2,16384]{2,1,0:T(2,128)(2,1)S(1)}, u32[]{:S(2)}, u32[]{:S(2)}) async-start(bf16[4,2,16384]{2,1,0:T(2,128)(2,1)} %all_to_all.28), calls=%async_computation.4 | async-start | bytes 524288 | tf_op jit(solution)/shard_map/all_to_all | solution.py:197
Sparse Core Ops, SparseCore 0:
  33.3 102.3 reduce-scatter.10
  141.0 98.6 reduce-scatter.8
  244.9 98.5 reduce-scatter.6
  348.7 98.6 reduce-scatter.4
